TPU v7x, 512 devices: a whole 4x4x16 slice. The times are simulated.
512 devices in a mesh: seq: 128 (over z, y, x_hi), branch: 4 (over x_lo, core).
Axes of the slice: x: 4 (x_hi: 2, x_lo: 2; x = x_hi * 2 + x_lo), y: 4, z: 16, core: 2. Of those that a mesh axis runs over, the one named last changes fastest.
Arguments:
- q_ctl: bfloat16 [4, 24576, 2048], P('branch', 'seq'), may hold values from -64 to 64
- k_ctl: bfloat16 [4, 24576, 2048], P('branch', 'seq'), may hold values from -64 to 64
- v_ctl: bfloat16 [4, 24576, 2048], P('branch', 'seq'), may hold values from -6 to 6
- positions: int32 [24576], P('seq'), may hold values from 0 to 12287
- branch_ids: int32 [4], P('branch'), may hold values from 0 to 63
- cond_scale: float32 [64], replicated, may hold values from 0.25 to 2
- out_weight: bfloat16 [2048, 3072], P('branch', 'seq'), may hold values from -0.125 to 0.125
- frozen: bfloat16 [24576, 3072], P(('seq', 'branch')), may hold values from -2.390625 to 2.390625
- norm_gain: float32 [3072], replicated, may hold values from 0.5 to 1.5
- cotangent: bfloat16 [24576, 3072], P('seq'), may hold values from -6 to 6
Outputs:
- normed: bfloat16 [24576, 3072], P(('seq', 'branch'))
- grad_attn: bfloat16 [4, 24576, 2048], P('branch', 'seq')
All inputs are finite; a program needn't handle non-finite values.
Results may differ from a plain program's by a relative error of at most 0.014.
Values may be sent and summed in bfloat16 or wider, within the bound.
No kernel may reach another device: no remote copies, remote signals or barrier semaphores. Data moves between devices by JAX's collectives and lax.ppermute only.
A program may use at most 64 MiB of HBM per device.

v0:
```python
import math
import jax
import jax.numpy as jnp
from jax import lax
from jax.sharding import PartitionSpec as P

HEADS = 16
HEAD_DIM = 128
EPS = 1e-06


def from_partner(shard, axis, distance):
    return lax.ppermute(shard, axis, [(i, i ^ 1 << distance) for i in range(lax.axis_size(axis))])


def rope_tables(positions, head_dim):
    exponents = jnp.arange(head_dim // 2, dtype=jnp.float32) * (2.0 / head_dim)
    frequencies = 10000.0 ** (-exponents)
    angles = positions.astype(jnp.float32)[..., None] * frequencies
    return (jnp.cos(angles), jnp.sin(angles))


def rotate(values_in, cosines, sines):
    half_dim = values_in.shape[-1] // 2
    front_half = values_in[..., :half_dim]
    back_half = values_in[..., half_dim:]
    return jnp.concatenate(
        [front_half * cosines - back_half * sines, back_half * cosines + front_half * sines],
        axis=-1,
    )


def normalize(hidden, norm_gain):
    inverse = lax.rsqrt(jnp.mean(hidden * hidden, axis=-1, keepdims=True) + EPS)
    return (hidden * inverse * norm_gain).astype(jnp.bfloat16)


def norm_grad(hidden, norm_gain, cotangent):
    inverse = lax.rsqrt(jnp.mean(hidden * hidden, axis=-1, keepdims=True) + EPS)
    upstream = cotangent.astype(jnp.float32) * norm_gain
    inner_mean = jnp.mean(upstream * hidden, axis=-1, keepdims=True)
    return (inverse * upstream - hidden * (inverse * inverse * inverse) * inner_mean).astype(
        jnp.bfloat16
    )


def attend_head(packed):
    query_rows, key_rows, value_rows = packed
    clip_len = query_rows.shape[0]
    block_rows = min(512, clip_len)
    factor = 1.0 / math.sqrt(query_rows.shape[-1])

    def one_block(query_block):
        scores = jnp.dot(query_block, key_rows.T, preferred_element_type=jnp.float32) * factor
        row_max = jnp.max(scores, axis=-1, keepdims=True)
        weights = jnp.exp(scores - row_max)
        row_total = jnp.sum(weights, axis=-1, keepdims=True)
        weights_low = (weights / row_total).astype(jnp.bfloat16)
        return jnp.dot(weights_low, value_rows, preferred_element_type=jnp.float32).astype(
            jnp.bfloat16
        )

    blocks = query_rows.reshape(clip_len // block_rows, block_rows, query_rows.shape[-1])
    return lax.map(one_block, blocks).reshape(clip_len, query_rows.shape[-1])


def regroup(buffer, group_bits, seq_index, forward):
    full_shape = buffer.shape
    split = buffer.reshape(full_shape[:1] + (2,) * group_bits + full_shape[2:])
    for bit in range(group_bits):
        axis_here = group_bits - bit
        mine = jnp.bitwise_and(jnp.right_shift(seq_index, bit), 1)
        other = 1 - mine
        outgoing = lax.dynamic_index_in_dim(split, other, axis_here, keepdims=True)
        if forward:
            incoming = from_partner(outgoing, "seq", bit)
        else:
            incoming = from_partner(outgoing, "seq", bit)
        split = lax.dynamic_update_index_in_dim(split, incoming, other, axis_here)
    return split.reshape(full_shape)


def on_device(
    q_ctl, k_ctl, v_ctl, positions, branch_ids, cond_scale, out_weight, frozen, norm_gain, cotangent
):
    branch_index = lax.axis_index("branch")
    quarters = lax.axis_size("branch")
    seq_index = lax.axis_index("seq")
    seq_devices = lax.axis_size("seq")
    group = min(HEADS, seq_devices)
    group_bits = group.bit_length() - 1
    local_len = q_ctl.shape[1]
    feature_width = q_ctl.shape[2]
    head_dim = HEAD_DIM
    head_count = feature_width // head_dim
    heads_here = head_count // group
    clip_len = group * local_len
    quarter_len = local_len // quarters
    model_width = cotangent.shape[1]
    cosines, sines = rope_tables(positions, head_dim)
    cosines = cosines[:, None, :]
    sines = sines[:, None, :]

    def heads_first(source, rotated):
        split_heads = source[0].reshape(local_len, head_count, head_dim)
        if rotated:
            split_heads = rotate(split_heads.astype(jnp.float32), cosines, sines).astype(
                jnp.bfloat16
            )
        split_heads = split_heads.reshape(local_len, group, heads_here, head_dim)
        return jnp.transpose(split_heads, (1, 0, 2, 3))

    stacked = jnp.stack(
        [heads_first(q_ctl, True), heads_first(k_ctl, True), heads_first(v_ctl, False)]
    )
    arrived = regroup(stacked, group_bits, seq_index, True)

    def per_head(member):
        return jnp.transpose(member, (2, 0, 1, 3)).reshape(heads_here, clip_len, head_dim)

    attended_heads = lax.map(
        attend_head, (per_head(arrived[0]), per_head(arrived[1]), per_head(arrived[2]))
    )
    going_back = jnp.transpose(
        attended_heads.reshape(heads_here, group, local_len, head_dim), (1, 2, 0, 3)
    )[None]
    returned = regroup(going_back, group_bits, seq_index, False)[0]
    attended = jnp.transpose(returned, (1, 0, 2, 3)).reshape(local_len, feature_width)
    branch_scale = jnp.sum(
        jnp.where(jnp.arange(cond_scale.shape[0]) == branch_ids[0], cond_scale, 0.0)
    )
    weight_rows = lax.all_gather(out_weight, "seq", axis=1, tiled=True)
    mixed = lax.psum_scatter(
        (branch_scale * attended.astype(jnp.float32)).astype(jnp.bfloat16),
        "branch",
        scatter_dimension=1,
        tiled=True,
    ).astype(jnp.float32)
    mixed_high = mixed.astype(jnp.bfloat16)
    mixed_rest = (mixed - mixed_high.astype(jnp.float32)).astype(jnp.bfloat16)
    partial_stream = jnp.dot(mixed_high, weight_rows, preferred_element_type=jnp.float32)
    partial_stream = partial_stream + jnp.dot(
        mixed_rest, weight_rows, preferred_element_type=jnp.float32
    )
    owner = (jnp.arange(quarters) == branch_index).astype(jnp.float32)[:, None, None]
    term = (
        partial_stream.reshape(quarters, quarter_len, model_width)
        + owner * frozen.astype(jnp.float32)[None]
    )
    hidden = (
        lax.psum(term.astype(jnp.bfloat16), "branch")
        .astype(jnp.float32)
        .reshape(local_len, model_width)
    )
    hidden_share = lax.dynamic_slice_in_dim(hidden, branch_index * quarter_len, quarter_len, 0)
    normed = normalize(hidden_share, norm_gain)
    grad_hidden = norm_grad(hidden, norm_gain, cotangent)
    cot_block = jnp.einsum(
        "td,hd->th", grad_hidden, weight_rows, preferred_element_type=jnp.float32
    ).astype(jnp.bfloat16)
    cot_attn = lax.all_gather(cot_block, "branch", axis=1, tiled=True)
    grad_attn = (branch_scale * cot_attn.astype(jnp.float32)).astype(jnp.bfloat16)
    return (normed, grad_attn.reshape(1, local_len, feature_width))


def solution(mesh):
    return jax.shard_map(
        on_device,
        mesh=mesh,
        in_specs=(
            P("branch", "seq", None),
            P("branch", "seq", None),
            P("branch", "seq", None),
            P("seq"),
            P("branch"),
            P(),
            P("branch", "seq"),
            P(("seq", "branch"), None),
            P(),
            P("seq", None),
        ),
        out_specs=(P(("seq", "branch"), None), P("branch", "seq", None)),
        check_vma=False,
    )
```

profile of v0, /device:TPU:1, one launch (start us, length us, event | category | flops | bytes accessed | tf_op | source)
XLA Modules:
  0.0 424.5 jit_solution(8821610244191821590)
XLA Ops:
  8.7 1.4 convert_bitcast_fusion.1
  11.3 1.1 fusion.16
  12.4 0.9 maximum_bitcast_fusion
  13.5 1.1 copy.15
  14.8 1.1 copy.17
  15.9 1.6 pad_maximum_fusion
  17.5 1.1 constant_dynamic-slice_fusion.7
  18.6 5.4 %collective-permute-start = (bf16[3,2,2,2,1,192,1,128]{7,5,4,3,2,1,6,0:T(8,128)(2,1)}, bf16[3,2,2,2,1,192,1,128]{7,5,4,3,2,1,6,0:T(8,128)(2,1)S(1)}, u32[]{:S(2)}, u32[]{:S(2)}) collective-permute-start(bf16[3,2,2,2,1,192,1,128]{7,5,4,3,2,1,6,0:T(8,128)(2,1)} %constant_dynamic-slice_fusion.7), channel_id=1, source_target_pairs={{0,4},{4,0},{8,12},{12,8},{16,20},{20,16},{24,28},{28,24},{32,36},... | collective-permute-start | bytes 3538952 | tf_op jit(solution)/shard_map/ppermute | solution.py:13
  24.1 22.6 %collective-permute-done = bf16[3,2,2,2,1,192,1,128]{7,5,4,3,2,1,6,0:T(8,128)(2,1)S(1)} collective-permute-done((bf16[3,2,2,2,1,192,1,128]{7,5,4,3,2,1,6,0:T(8,128)(2,1)}, bf16[3,2,2,2,1,192,1,128]{7,5,4,3,2,1,6,0:T(8,128)(2,1)S(1)}, u32[]{:S(2)}, u32[]{:S(2)}) %collective-permute-start) | collective-permute-done | bytes 1179680 | tf_op jit(solution)/shard_map/ppermute | solution.py:13
  46.8 1.1 constant_dynamic-slice_fusion.6
  47.9 6.5 %collective-permute-start.1 = (bf16[3,2,2,1,2,192,1,128]{7,5,4,3,2,1,6,0:T(8,128)(2,1)}, bf16[3,2,2,1,2,192,1,128]{7,5,4,3,2,1,6,0:T(8,128)(2,1)S(1)}, u32[]{:S(2)}, u32[]{:S(2)}) collective-permute-start(bf16[3,2,2,1,2,192,1,128]{7,5,4,3,2,1,6,0:T(8,128)(2,1)} %constant_dynamic-slice_fusion.6), channel_id=1, source_target_pairs={{0,8},{4,12},{8,0},{12,4},{16,24},{20,28},{24,16},{28,20},{32,40},... | collective-permute-start | bytes 3538952 | tf_op jit(solution)/shard_map/ppermute | solution.py:13
  54.4 24.8 %collective-permute-done.1 = bf16[3,2,2,1,2,192,1,128]{7,5,4,3,2,1,6,0:T(8,128)(2,1)S(1)} collective-permute-done((bf16[3,2,2,1,2,192,1,128]{7,5,4,3,2,1,6,0:T(8,128)(2,1)}, bf16[3,2,2,1,2,192,1,128]{7,5,4,3,2,1,6,0:T(8,128)(2,1)S(1)}, u32[]{:S(2)}, u32[]{:S(2)}) %collective-permute-start.1) | collective-permute-done | bytes 1179680 | tf_op jit(solution)/shard_map/ppermute | solution.py:13
  79.4 1.1 constant_dynamic-slice_fusion.5
  80.5 4.9 %collective-permute-start.2 = (bf16[3,2,1,2,2,192,1,128]{7,5,4,3,2,1,6,0:T(8,128)(2,1)}, bf16[3,2,1,2,2,192,1,128]{7,5,4,3,2,1,6,0:T(8,128)(2,1)S(1)}, u32[]{:S(2)}, u32[]{:S(2)}) collective-permute-start(bf16[3,2,1,2,2,192,1,128]{7,5,4,3,2,1,6,0:T(8,128)(2,1)} %constant_dynamic-slice_fusion.5), channel_id=1, source_target_pairs={{0,16},{4,20},{8,24},{12,28},{16,0},{20,4},{24,8},{28,12},{32,48},... | collective-permute-start | bytes 3538952 | tf_op jit(solution)/shard_map/ppermute | solution.py:13
  85.4 24.0 %collective-permute-done.2 = bf16[3,2,1,2,2,192,1,128]{7,5,4,3,2,1,6,0:T(8,128)(2,1)S(1)} collective-permute-done((bf16[3,2,1,2,2,192,1,128]{7,5,4,3,2,1,6,0:T(8,128)(2,1)}, bf16[3,2,1,2,2,192,1,128]{7,5,4,3,2,1,6,0:T(8,128)(2,1)S(1)}, u32[]{:S(2)}, u32[]{:S(2)}) %collective-permute-start.2) | collective-permute-done | bytes 1179680 | tf_op jit(solution)/shard_map/ppermute | solution.py:13
  109.6 1.2 constant_dynamic-slice_fusion.4
  110.8 3.5 collective-permute-start.3
  114.3 23.2 %collective-permute-done.3 = bf16[3,1,2,2,2,192,1,128]{7,5,4,3,2,1,6,0:T(8,128)(2,1)S(1)} collective-permute-done((bf16[3,1,2,2,2,192,1,128]{7,5,4,3,2,1,6,0:T(8,128)(2,1)}, bf16[3,1,2,2,2,192,1,128]{7,5,4,3,2,1,6,0:T(8,128)(2,1)S(1)}, u32[]{:S(2)}, u32[]{:S(2)}) %collective-permute-start.3) | collective-permute-done | bytes 1179680 | tf_op jit(solution)/shard_map/ppermute | solution.py:13
  137.7 1.4 fusion.22
  139.0 31.2 %while.17 = (s32[]{:T(128)}, bf16[6,512,128]{2,1,0:T(8,128)(2,1)}, bf16[6,512,128]{2,1,0:T(8,128)(2,1)}, bf16[3072,128]{1,0:T(8,128)(2,1)S(1)}, bf16[3072,128]{1,0:T(8,128)(2,1)}, /*index=5*/s32[]{:T(128)}) while((s32[]{:T(128)}, bf16[6,512,128]{2,1,0:T(8,128)(2,1)}, bf16[6,512,128]{2,1,0:T(8,128)(2,1)}, bf16[3072,128]{1,0:T(8,128)(2,1)S(1)}, ...), condition=%wide.region_4.5_spmd, body=%wide.region_1.4_spmd.sunk | while | flops 819526656 | bytes 23866464 | solution.py:64
  139.0 2.0 multiply_reduce_fusion.5
  141.0 1.2 fusion.36
  142.2 2.1 fusion.37
  144.2 2.0 multiply_reduce_fusion.5
  146.2 1.2 fusion.36
  147.4 2.1 fusion.37
  149.4 2.0 multiply_reduce_fusion.5
  151.4 1.2 fusion.36
  152.6 2.1 fusion.37
  154.6 2.0 multiply_reduce_fusion.5
  156.6 1.2 fusion.36
  157.8 2.1 fusion.37
  159.8 2.0 multiply_reduce_fusion.5
  161.8 1.2 fusion.36
  163.0 2.1 fusion.37
  165.0 2.0 multiply_reduce_fusion.5
  167.0 1.2 fusion.36
  168.2 2.1 fusion.37
  170.2 1.0 constant_dynamic-slice_fusion.3
  171.3 4.6 %collective-permute-start.4 = (bf16[1,2,2,2,1,192,1,128]{7,5,4,3,2,1,6,0:T(8,128)(2,1)S(1)}, bf16[1,2,2,2,1,192,1,128]{7,5,4,3,2,1,6,0:T(8,128)(2,1)S(1)}, u32[]{:S(2)}, u32[]{:S(2)}) collective-permute-start(bf16[1,2,2,2,1,192,1,128]{7,5,4,3,2,1,6,0:T(8,128)(2,1)S(1)} %constant_dynamic-slice_fusion.3), channel_id=1, source_target_pairs={{0,4},{4,0},{8,12},{12,8},{16,20},{20,16},{24,28},{28,24},{32,36},... | collective-permute-start | bytes 1179656 | tf_op jit(solution)/shard_map/ppermute | solution.py:13
  175.9 5.4 %collective-permute-done.4 = bf16[1,2,2,2,1,192,1,128]{7,5,4,3,2,1,6,0:T(8,128)(2,1)S(1)} collective-permute-done((bf16[1,2,2,2,1,192,1,128]{7,5,4,3,2,1,6,0:T(8,128)(2,1)S(1)}, bf16[1,2,2,2,1,192,1,128]{7,5,4,3,2,1,6,0:T(8,128)(2,1)S(1)}, u32[]{:S(2)}, u32[]{:S(2)}) %collective-permute-start.4) | collective-permute-done | bytes 393248 | tf_op jit(solution)/shard_map/ppermute | solution.py:13
  182.1 1.0 constant_dynamic-slice_fusion.2
  183.2 3.2 collective-permute-start.5
  186.3 5.7 %collective-permute-done.5 = bf16[1,2,2,1,2,192,1,128]{7,5,4,3,2,1,6,0:T(8,128)(2,1)S(1)} collective-permute-done((bf16[1,2,2,1,2,192,1,128]{7,5,4,3,2,1,6,0:T(8,128)(2,1)S(1)}, bf16[1,2,2,1,2,192,1,128]{7,5,4,3,2,1,6,0:T(8,128)(2,1)S(1)}, u32[]{:S(2)}, u32[]{:S(2)}) %collective-permute-start.5) | collective-permute-done | bytes 393248 | tf_op jit(solution)/shard_map/ppermute | solution.py:13
  192.1 0.8 constant_dynamic-update-slice_fusion.2
  192.9 1.0 constant_dynamic-slice_fusion.1
  193.9 4.8 %collective-permute-start.6 = (bf16[1,2,1,2,2,192,1,128]{7,5,4,3,2,1,6,0:T(8,128)(2,1)S(1)}, bf16[1,2,1,2,2,192,1,128]{7,5,4,3,2,1,6,0:T(8,128)(2,1)S(1)}, u32[]{:S(2)}, u32[]{:S(2)}) collective-permute-start(bf16[1,2,1,2,2,192,1,128]{7,5,4,3,2,1,6,0:T(8,128)(2,1)S(1)} %constant_dynamic-slice_fusion.1), channel_id=1, source_target_pairs={{0,16},{4,20},{8,24},{12,28},{16,0},{20,4},{24,8},{28,12},{32,48},... | collective-permute-start | bytes 1179656 | tf_op jit(solution)/shard_map/ppermute | solution.py:13
  198.7 5.2 %collective-permute-done.6 = bf16[1,2,1,2,2,192,1,128]{7,5,4,3,2,1,6,0:T(8,128)(2,1)S(1)} collective-permute-done((bf16[1,2,1,2,2,192,1,128]{7,5,4,3,2,1,6,0:T(8,128)(2,1)S(1)}, bf16[1,2,1,2,2,192,1,128]{7,5,4,3,2,1,6,0:T(8,128)(2,1)S(1)}, u32[]{:S(2)}, u32[]{:S(2)}) %collective-permute-start.6) | collective-permute-done | bytes 393248 | tf_op jit(solution)/shard_map/ppermute | solution.py:13
  204.8 1.0 constant_dynamic-slice_fusion
  205.8 3.5 collective-permute-start.7
  210.6 4.3 %collective-permute-done.7 = bf16[1,1,2,2,2,192,1,128]{7,5,4,3,2,1,6,0:T(8,128)(2,1)S(1)} collective-permute-done((bf16[1,1,2,2,2,192,1,128]{7,5,4,3,2,1,6,0:T(8,128)(2,1)S(1)}, bf16[1,1,2,2,2,192,1,128]{7,5,4,3,2,1,6,0:T(8,128)(2,1)S(1)}, u32[]{:S(2)}, u32[]{:S(2)}) %collective-permute-start.7) | collective-permute-done | bytes 393248 | tf_op jit(solution)/shard_map/ppermute | solution.py:13
  215.6 2.0 multiply_convert_fusion.1
  218.4 1.1 copy.24
  219.6 0.9 convert_element_type.103
  220.4 109.9 %all-gather.2.cloned.1.call-done = bf16[512,3072]{0,1:T(8,128)(2,1)} async-done(((bf16[512,24]{0,1:T(8,128)(2,1)}), bf16[512,3072]{0,1:T(8,128)(2,1)}) %all-gather.2.cloned.1.call-update) | async-done | bytes 3145744 | tf_op jit(solution)/shard_map/all_gather | solution.py:132
  330.4 3.3 fusion.23
  333.7 1.2 convolution_add_fusion
  334.9 1.3 add_convert_fusion
  336.3 62.4 %all-reduce.2.cloned.1.call-done = bf16[4,48,3072]{2,1,0:T(8,128)(2,1)} async-done(((bf16[4,48,3072]{2,1,0:T(8,128)(2,1)}), bf16[4,48,3072]{2,1,0:T(8,128)(2,1)}) %all-reduce.2.cloned.1.call-update) | async-done | bytes 1179664 | tf_op jit(solution)/shard_map/psum | solution.py:151
  398.7 3.5 multiply_reduce_fusion.1
  402.7 2.8 fusion.15
  405.5 8.8 %all_gather.7 = bf16[192,2048]{1,0:T(8,128)(2,1)S(1)} all-gather(bf16[192,512]{1,0:T(8,128)(2,1)S(1)} %fusion.15), channel_id=1, replica_groups=mesh['seq'=128,'branch'=4] {'branch'}, dimensions={1}, use_global_device_ids=true | all-gather | bytes 983040 | tf_op jit(solution)/shard_map/all_gather | solution.py:161
  414.4 1.7 fusion.20
  416.2 0.8 multiply_convert_fusion.2
  (65 shorter events, 7.6 us)
Async XLA Ops:
  8.0 322.4 %all-gather.2.cloned.1.call-start = ((), (), s32[]{:S(2)}) async-start(), calls=%async_computation.2 | async-start | bytes 3170304 | tf_op jit(solution)/shard_map/all_gather | solution.py:132
  8.7 1.7 copy-start.7
  13.3 1.3 copy-start.6
  18.6 28.0 %collective-permute-start = (bf16[3,2,2,2,1,192,1,128]{7,5,4,3,2,1,6,0:T(8,128)(2,1)}, bf16[3,2,2,2,1,192,1,128]{7,5,4,3,2,1,6,0:T(8,128)(2,1)S(1)}, u32[]{:S(2)}, u32[]{:S(2)}) collective-permute-start(bf16[3,2,2,2,1,192,1,128]{7,5,4,3,2,1,6,0:T(8,128)(2,1)} %constant_dynamic-slice_fusion.7), channel_id=1, source_target_pairs={{0,4},{4,0},{8,12},{12,8},{16,20},{20,16},{24,28},{28,24},{32,36},... | collective-permute-start | bytes 3538952 | tf_op jit(solution)/shard_map/ppermute | solution.py:13
  47.9 31.3 %collective-permute-start.1 = (bf16[3,2,2,1,2,192,1,128]{7,5,4,3,2,1,6,0:T(8,128)(2,1)}, bf16[3,2,2,1,2,192,1,128]{7,5,4,3,2,1,6,0:T(8,128)(2,1)S(1)}, u32[]{:S(2)}, u32[]{:S(2)}) collective-permute-start(bf16[3,2,2,1,2,192,1,128]{7,5,4,3,2,1,6,0:T(8,128)(2,1)} %constant_dynamic-slice_fusion.6), channel_id=1, source_target_pairs={{0,8},{4,12},{8,0},{12,4},{16,24},{20,28},{24,16},{28,20},{32,40},... | collective-permute-start | bytes 3538952 | tf_op jit(solution)/shard_map/ppermute | solution.py:13
  80.5 28.9 %collective-permute-start.2 = (bf16[3,2,1,2,2,192,1,128]{7,5,4,3,2,1,6,0:T(8,128)(2,1)}, bf16[3,2,1,2,2,192,1,128]{7,5,4,3,2,1,6,0:T(8,128)(2,1)S(1)}, u32[]{:S(2)}, u32[]{:S(2)}) collective-permute-start(bf16[3,2,1,2,2,192,1,128]{7,5,4,3,2,1,6,0:T(8,128)(2,1)} %constant_dynamic-slice_fusion.5), channel_id=1, source_target_pairs={{0,16},{4,20},{8,24},{12,28},{16,0},{20,4},{24,8},{28,12},{32,48},... | collective-permute-start | bytes 3538952 | tf_op jit(solution)/shard_map/ppermute | solution.py:13
  110.8 26.7 %collective-permute-start.3 = (bf16[3,1,2,2,2,192,1,128]{7,5,4,3,2,1,6,0:T(8,128)(2,1)}, bf16[3,1,2,2,2,192,1,128]{7,5,4,3,2,1,6,0:T(8,128)(2,1)S(1)}, u32[]{:S(2)}, u32[]{:S(2)}) collective-permute-start(bf16[3,1,2,2,2,192,1,128]{7,5,4,3,2,1,6,0:T(8,128)(2,1)} %constant_dynamic-slice_fusion.4), channel_id=1, source_target_pairs={{0,32},{4,36},{8,40},{12,44},{16,48},{20,52},{24,56},{28,60},{32,0... | collective-permute-start | bytes 3538952 | tf_op jit(solution)/shard_map/ppermute | solution.py:13
  114.3 216.1 %reduce-scatter.2.cloned.1.call-start = ((), (), s32[]{:S(2)}) async-start(), calls=%async_computation.1 | async-start | bytes 983040 | tf_op jit(solution)/shard_map/reduce_scatter | solution.py:133
  141.0 1.2 copy-start.4
  146.2 1.2 copy-start.4
  151.4 1.2 copy-start.4
  156.6 1.2 copy-start.4
  161.8 1.2 copy-start.4
  167.0 1.2 copy-start.4
  171.3 38.6 %copy-start.10 = (f32[64]{0:T(128)S(1)}, f32[64]{0:T(128)}, u32[]{:S(2)}) copy-start(f32[64]{0:T(128)} %param.17) | copy-start | bytes 772
  171.3 10.0 %collective-permute-start.4 = (bf16[1,2,2,2,1,192,1,128]{7,5,4,3,2,1,6,0:T(8,128)(2,1)S(1)}, bf16[1,2,2,2,1,192,1,128]{7,5,4,3,2,1,6,0:T(8,128)(2,1)S(1)}, u32[]{:S(2)}, u32[]{:S(2)}) collective-permute-start(bf16[1,2,2,2,1,192,1,128]{7,5,4,3,2,1,6,0:T(8,128)(2,1)S(1)} %constant_dynamic-slice_fusion.3), channel_id=1, source_target_pairs={{0,4},{4,0},{8,12},{12,8},{16,20},{20,16},{24,28},{28,24},{32,36},... | collective-permute-start | bytes 1179656 | tf_op jit(solution)/shard_map/ppermute | solution.py:13
  183.2 8.9 %collective-permute-start.5 = (bf16[1,2,2,1,2,192,1,128]{7,5,4,3,2,1,6,0:T(8,128)(2,1)S(1)}, bf16[1,2,2,1,2,192,1,128]{7,5,4,3,2,1,6,0:T(8,128)(2,1)S(1)}, u32[]{:S(2)}, u32[]{:S(2)}) collective-permute-start(bf16[1,2,2,1,2,192,1,128]{7,5,4,3,2,1,6,0:T(8,128)(2,1)S(1)} %constant_dynamic-slice_fusion.2), channel_id=1, source_target_pairs={{0,8},{4,12},{8,0},{12,4},{16,24},{20,28},{24,16},{28,20},{32,40},... | collective-permute-start | bytes 1179656 | tf_op jit(solution)/shard_map/ppermute | solution.py:13
  193.9 10.0 %collective-permute-start.6 = (bf16[1,2,1,2,2,192,1,128]{7,5,4,3,2,1,6,0:T(8,128)(2,1)S(1)}, bf16[1,2,1,2,2,192,1,128]{7,5,4,3,2,1,6,0:T(8,128)(2,1)S(1)}, u32[]{:S(2)}, u32[]{:S(2)}) collective-permute-start(bf16[1,2,1,2,2,192,1,128]{7,5,4,3,2,1,6,0:T(8,128)(2,1)S(1)} %constant_dynamic-slice_fusion.1), channel_id=1, source_target_pairs={{0,16},{4,20},{8,24},{12,28},{16,0},{20,4},{24,8},{28,12},{32,48},... | collective-permute-start | bytes 1179656 | tf_op jit(solution)/shard_map/ppermute | solution.py:13
  205.8 9.1 %collective-permute-start.7 = (bf16[1,1,2,2,2,192,1,128]{7,5,4,3,2,1,6,0:T(8,128)(2,1)S(1)}, bf16[1,1,2,2,2,192,1,128]{7,5,4,3,2,1,6,0:T(8,128)(2,1)S(1)}, u32[]{:S(2)}, u32[]{:S(2)}) collective-permute-start(bf16[1,1,2,2,2,192,1,128]{7,5,4,3,2,1,6,0:T(8,128)(2,1)S(1)} %constant_dynamic-slice_fusion), channel_id=1, source_target_pairs={{0,32},{4,36},{8,40},{12,44},{16,48},{20,52},{24,56},{28,60},{32,0... | collective-permute-start | bytes 1179656 | tf_op jit(solution)/shard_map/ppermute | solution.py:13
  217.6 2.0 copy-start.8
  219.5 179.2 %all-reduce.2.cloned.1.call-start = ((), (), s32[]{:S(2)}) async-start(), calls=%async_computation.3 | async-start | bytes 2359296 | tf_op jit(solution)/shard_map/psum | solution.py:151
  330.4 3.3 copy-start
  330.4 3.3 copy-start.5
  333.7 1.2 copy-start.3
  334.9 63.8 %copy-start.9 = (f32[3072]{0:T(1024)S(1)}, f32[3072]{0:T(1024)}, u32[]{:S(2)}) copy-start(f32[3072]{0:T(1024)} %param.20) | copy-start | bytes 36868
  398.7 3.5 copy-start.2
  405.5 10.5 %copy-start.1 = (f32[192,3072]{1,0:T(8,128)S(1)}, f32[192,3072]{1,0:T(8,128)}, u32[]{:S(2)}) copy-start(f32[192,3072]{1,0:T(8,128)} %get-tuple-element.56) | copy-start | bytes 7077892
Sparse Core Ops, SparseCore 0:
  114.4 215.9 all-gather.1
Sparse Core Ops, SparseCore 1:
  219.6 39.7 reduce-scatter.1
  336.4 62.3 all-reduce.1
where the time goes:
time: 425 us; the launch traced here: 424 us
  waiting for transfers between devices  288 us (68%)
  starting transfers between devices  36.4 us (9%)
  matrix products  31.5 us (7%)
  other arithmetic  24.5 us (6%)
  local copies, waits for them, and re-layouts  19.1 us (4%)
  between operations  16.5 us (4%)
  blocking collectives  8.84 us (2%)
    ppermute x8, waiting for transfers between devices, from_partner(): lax.ppermute(shard, axis, [(i, i ^ 1 << distance) for i in range(lax.axis...  115 us
    all_gather x1, waiting for transfers between devices, on_device(): weight_rows = lax.all_gather(out_weight, 'seq', axis=1, tiled=True)  110 us
    psum x1, waiting for transfers between devices, on_device(): lax.psum(term.astype(jnp.bfloat16), 'branch').astype(jnp.float32)  62.4 us
    ppermute x8, starting transfers between devices, from_partner(): lax.ppermute(shard, axis, [(i, i ^ 1 << distance) for i in range(lax.axis...  36.3 us
    dot_general x6, matrix products, one_block(): jnp.dot(weights_low, value_rows, preferred_element_type=jnp.float32)  12.4 us
    dot_general x6, matrix products, one_block(): jnp.dot(query_block, key_rows.T, preferred_element_type=jnp.float32)  11.8 us
    all_gather x1, blocking collectives, on_device(): cot_attn = lax.all_gather(cot_block, 'branch', axis=1, tiled=True)  8.84 us
    dynamic_slice x8, local copies, waits for them, and re-layouts, regroup(): outgoing = lax.dynamic_index_in_dim(split, other, axis_here, keepdims=True)  8.65 us
  transfers between devices with their start and end apart: 11, of which 10 were waited for; matrix products, arithmetic and copies ran while one was open for 11% of the time, Pallas kernels for 0%

commit v1 on v0

--- a/solution.py
+++ b/solution.py
@@ -129,7 +129,8 @@
     branch_scale = jnp.sum(
         jnp.where(jnp.arange(cond_scale.shape[0]) == branch_ids[0], cond_scale, 0.0)
     )
-    weight_rows = lax.all_gather(out_weight, "seq", axis=1, tiled=True)
+    stack = jnp.stack([out_weight] * lax.axis_size("seq"))
+    weight_rows = jnp.concatenate(lax.all_to_all(stack, "seq", 0, 0), axis=1)
     mixed = lax.psum_scatter(
         (branch_scale * attended.astype(jnp.float32)).astype(jnp.bfloat16),
         "branch",

time: 425 us -> 413 us (0.972)
  waiting for transfers between devices: 288 us -> 256 us
  starting transfers between devices: 36.4 us -> 53.8 us
    all_gather x1 -> x0, waiting for transfers between devices: 110 us -> none  [on_device(): weight_rows = lax.all_gather(out_weight, 'seq', axis=1, tiled=True)]
    ppermute x8, waiting for transfers between devices: 115 us -> 162 us  [from_partner(): lax.ppermute(shard, axis, [(i, i ^ 1 << distance) for i in range(lax.axis...]
    reduce_scatter x1, waiting for transfers between devices: 0.01 us -> 34.9 us  [on_device(): lax.psum_scatter((branch_scale * attended.astype(jnp.float32)).astype(jnp...]
    all_to_all x0 -> x1, starting transfers between devices: none -> 21.7 us  [on_device(): weight_rows = jnp.concatenate(lax.all_to_all(stack, 'seq', 0, 0), axis=1)]
    ppermute x8, starting transfers between devices: 36.3 us -> 31.9 us  [from_partner(): lax.ppermute(shard, axis, [(i, i ^ 1 << distance) for i in range(lax.axis...]
  transfers between devices with their start and end apart: 11 -> 11, of which waited for: 10 -> 9; matrix products, arithmetic and copies ran while one was open for 11% -> 11% of each run, Pallas kernels for 0% -> 0%
where the time goes in v1:
time: 413 us; the launch traced here: 411 us
  waiting for transfers between devices  256 us (62%)
  starting transfers between devices  53.8 us (13%)
  matrix products  33.3 us (8%)
  other arithmetic  23.1 us (6%)
  local copies, waits for them, and re-layouts  21.6 us (5%)
  between operations  15.1 us (4%)
  blocking collectives  8.71 us (2%)
    ppermute x8, waiting for transfers between devices, from_partner(): lax.ppermute(shard, axis, [(i, i ^ 1 << distance) for i in range(lax.axis...  162 us
    psum x1, waiting for transfers between devices, on_device(): lax.psum(term.astype(jnp.bfloat16), 'branch').astype(jnp.float32)  59.1 us
    reduce_scatter x1, waiting for transfers between devices, on_device(): lax.psum_scatter((branch_scale * attended.astype(jnp.float32)).astype(jnp...  34.9 us
    ppermute x8, starting transfers between devices, from_partner(): lax.ppermute(shard, axis, [(i, i ^ 1 << distance) for i in range(lax.axis...  31.9 us
    all_to_all x1, starting transfers between devices, on_device(): weight_rows = jnp.concatenate(lax.all_to_all(stack, 'seq', 0, 0), axis=1)  21.7 us
    dot_general x6, matrix products, one_block(): jnp.dot(weights_low, value_rows, preferred_element_type=jnp.float32)  12.4 us
    dot_general x6, matrix products, one_block(): jnp.dot(query_block, key_rows.T, preferred_element_type=jnp.float32)  11.8 us
    all_gather x1, blocking collectives, on_device(): cot_attn = lax.all_gather(cot_block, 'branch', axis=1, tiled=True)  8.71 us
  transfers between devices with their start and end apart: 11, of which 9 were waited for; matrix products, arithmetic and copies ran while one was open for 11% of the time, Pallas kernels for 0%

profile of v1, /device:TPU:1, one launch (start us, length us, event | category | flops | bytes accessed | tf_op | source)
XLA Modules:
  0.0 411.5 jit_solution(10611426497792304768)
XLA Ops:
  7.9 1.4 convert_bitcast_fusion.1
  10.4 1.1 fusion.16
  11.5 0.9 maximum_bitcast_fusion
  12.6 1.1 copy.16
  13.9 1.1 copy.18
  15.0 1.6 pad_maximum_fusion
  16.6 1.1 constant_dynamic-slice_fusion.7
  17.7 5.4 %collective-permute-start = (bf16[3,2,2,2,1,192,1,128]{7,5,4,3,2,1,6,0:T(8,128)(2,1)}, bf16[3,2,2,2,1,192,1,128]{7,5,4,3,2,1,6,0:T(8,128)(2,1)S(1)}, u32[]{:S(2)}, u32[]{:S(2)}) collective-permute-start(bf16[3,2,2,2,1,192,1,128]{7,5,4,3,2,1,6,0:T(8,128)(2,1)} %constant_dynamic-slice_fusion.7), channel_id=1, source_target_pairs={{0,4},{4,0},{8,12},{12,8},{16,20},{20,16},{24,28},{28,24},{32,36},... | collective-permute-start | bytes 3538952 | tf_op jit(solution)/shard_map/ppermute | solution.py:13
  23.2 22.6 %collective-permute-done = bf16[3,2,2,2,1,192,1,128]{7,5,4,3,2,1,6,0:T(8,128)(2,1)S(1)} collective-permute-done((bf16[3,2,2,2,1,192,1,128]{7,5,4,3,2,1,6,0:T(8,128)(2,1)}, bf16[3,2,2,2,1,192,1,128]{7,5,4,3,2,1,6,0:T(8,128)(2,1)S(1)}, u32[]{:S(2)}, u32[]{:S(2)}) %collective-permute-start) | collective-permute-done | bytes 1179680 | tf_op jit(solution)/shard_map/ppermute | solution.py:13
  45.9 1.1 constant_dynamic-slice_fusion.6
  47.1 6.5 %collective-permute-start.1 = (bf16[3,2,2,1,2,192,1,128]{7,5,4,3,2,1,6,0:T(8,128)(2,1)}, bf16[3,2,2,1,2,192,1,128]{7,5,4,3,2,1,6,0:T(8,128)(2,1)S(1)}, u32[]{:S(2)}, u32[]{:S(2)}) collective-permute-start(bf16[3,2,2,1,2,192,1,128]{7,5,4,3,2,1,6,0:T(8,128)(2,1)} %constant_dynamic-slice_fusion.6), channel_id=1, source_target_pairs={{0,8},{4,12},{8,0},{12,4},{16,24},{20,28},{24,16},{28,20},{32,40},... | collective-permute-start | bytes 3538952 | tf_op jit(solution)/shard_map/ppermute | solution.py:13
  53.5 24.8 %collective-permute-done.1 = bf16[3,2,2,1,2,192,1,128]{7,5,4,3,2,1,6,0:T(8,128)(2,1)S(1)} collective-permute-done((bf16[3,2,2,1,2,192,1,128]{7,5,4,3,2,1,6,0:T(8,128)(2,1)}, bf16[3,2,2,1,2,192,1,128]{7,5,4,3,2,1,6,0:T(8,128)(2,1)S(1)}, u32[]{:S(2)}, u32[]{:S(2)}) %collective-permute-start.1) | collective-permute-done | bytes 1179680 | tf_op jit(solution)/shard_map/ppermute | solution.py:13
  78.5 1.1 constant_dynamic-slice_fusion.5
  79.7 4.9 %collective-permute-start.2 = (bf16[3,2,1,2,2,192,1,128]{7,5,4,3,2,1,6,0:T(8,128)(2,1)}, bf16[3,2,1,2,2,192,1,128]{7,5,4,3,2,1,6,0:T(8,128)(2,1)S(1)}, u32[]{:S(2)}, u32[]{:S(2)}) collective-permute-start(bf16[3,2,1,2,2,192,1,128]{7,5,4,3,2,1,6,0:T(8,128)(2,1)} %constant_dynamic-slice_fusion.5), channel_id=1, source_target_pairs={{0,16},{4,20},{8,24},{12,28},{16,0},{20,4},{24,8},{28,12},{32,48},... | collective-permute-start | bytes 3538952 | tf_op jit(solution)/shard_map/ppermute | solution.py:13
  84.6 24.0 %collective-permute-done.2 = bf16[3,2,1,2,2,192,1,128]{7,5,4,3,2,1,6,0:T(8,128)(2,1)S(1)} collective-permute-done((bf16[3,2,1,2,2,192,1,128]{7,5,4,3,2,1,6,0:T(8,128)(2,1)}, bf16[3,2,1,2,2,192,1,128]{7,5,4,3,2,1,6,0:T(8,128)(2,1)S(1)}, u32[]{:S(2)}, u32[]{:S(2)}) %collective-permute-start.2) | collective-permute-done | bytes 1179680 | tf_op jit(solution)/shard_map/ppermute | solution.py:13
  108.7 1.2 constant_dynamic-slice_fusion.4
  109.9 3.5 collective-permute-start.3
  113.4 1.9 stack.14
  115.3 21.7 %all-to-all-start = ((bf16[128,512,24]{1,2,0:T(8,128)(2,1)}), bf16[128,512,24]{1,2,0:T(8,128)(2,1)}, u32[]{:S(2)}, u32[]{:S(2)}) async-start(bf16[128,512,24]{1,2,0:T(8,128)(2,1)} %stack.14), calls=%async_computation.1 | async-start | bytes 6291456 | tf_op jit(solution)/shard_map/all_to_all | solution.py:133
  137.4 1.4 fusion.22
  138.7 31.2 %while.17 = (s32[]{:T(128)}, bf16[6,512,128]{2,1,0:T(8,128)(2,1)}, bf16[6,512,128]{2,1,0:T(8,128)(2,1)}, bf16[3072,128]{1,0:T(8,128)(2,1)S(1)}, bf16[3072,128]{1,0:T(8,128)(2,1)}, /*index=5*/s32[]{:T(128)}) while((s32[]{:T(128)}, bf16[6,512,128]{2,1,0:T(8,128)(2,1)}, bf16[6,512,128]{2,1,0:T(8,128)(2,1)}, bf16[3072,128]{1,0:T(8,128)(2,1)S(1)}, ...), condition=%wide.region_4.5_spmd, body=%wide.region_1.4_spmd.sunk | while | flops 819526656 | bytes 23866464 | solution.py:64
  138.7 2.0 multiply_reduce_fusion.5
  140.7 1.2 fusion.36
  141.9 2.1 fusion.37
  144.0 2.0 multiply_reduce_fusion.5
  145.9 1.2 fusion.36
  147.1 2.1 fusion.37
  149.2 2.0 multiply_reduce_fusion.5
  151.1 1.2 fusion.36
  152.3 2.1 fusion.37
  154.4 2.0 multiply_reduce_fusion.5
  156.3 1.2 fusion.36
  157.5 2.1 fusion.37
  159.6 2.0 multiply_reduce_fusion.5
  161.5 1.2 fusion.36
  162.7 2.1 fusion.37
  164.8 2.0 multiply_reduce_fusion.5
  166.7 1.2 fusion.36
  167.9 2.1 fusion.37
  170.0 1.0 constant_dynamic-slice_fusion.3
  171.0 4.0 collective-permute-start.4
  175.1 7.7 %collective-permute-done.4 = bf16[1,2,2,2,1,192,1,128]{7,5,4,3,2,1,6,0:T(8,128)(2,1)S(1)} collective-permute-done((bf16[1,2,2,2,1,192,1,128]{7,5,4,3,2,1,6,0:T(8,128)(2,1)S(1)}, bf16[1,2,2,2,1,192,1,128]{7,5,4,3,2,1,6,0:T(8,128)(2,1)S(1)}, u32[]{:S(2)}, u32[]{:S(2)}) %collective-permute-start.4) | collective-permute-done | bytes 393248 | tf_op jit(solution)/shard_map/ppermute | solution.py:13
  183.6 1.0 constant_dynamic-slice_fusion.2
  184.6 2.8 collective-permute-start.5
  187.4 7.6 %collective-permute-done.5 = bf16[1,2,2,1,2,192,1,128]{7,5,4,3,2,1,6,0:T(8,128)(2,1)S(1)} collective-permute-done((bf16[1,2,2,1,2,192,1,128]{7,5,4,3,2,1,6,0:T(8,128)(2,1)S(1)}, bf16[1,2,2,1,2,192,1,128]{7,5,4,3,2,1,6,0:T(8,128)(2,1)S(1)}, u32[]{:S(2)}, u32[]{:S(2)}) %collective-permute-start.5) | collective-permute-done | bytes 393248 | tf_op jit(solution)/shard_map/ppermute | solution.py:13
  195.0 0.8 constant_dynamic-update-slice_fusion.2
  195.9 1.0 constant_dynamic-slice_fusion.1
  196.9 2.9 collective-permute-start.6
  199.8 9.4 %collective-permute-done.6 = bf16[1,2,1,2,2,192,1,128]{7,5,4,3,2,1,6,0:T(8,128)(2,1)S(1)} collective-permute-done((bf16[1,2,1,2,2,192,1,128]{7,5,4,3,2,1,6,0:T(8,128)(2,1)S(1)}, bf16[1,2,1,2,2,192,1,128]{7,5,4,3,2,1,6,0:T(8,128)(2,1)S(1)}, u32[]{:S(2)}, u32[]{:S(2)}) %collective-permute-start.6) | collective-permute-done | bytes 393248 | tf_op jit(solution)/shard_map/ppermute | solution.py:13
  210.0 1.0 constant_dynamic-slice_fusion
  211.1 1.9 collective-permute-start.7
  214.3 65.7 %collective-permute-done.7 = bf16[1,1,2,2,2,192,1,128]{7,5,4,3,2,1,6,0:T(8,128)(2,1)S(1)} collective-permute-done((bf16[1,1,2,2,2,192,1,128]{7,5,4,3,2,1,6,0:T(8,128)(2,1)S(1)}, bf16[1,1,2,2,2,192,1,128]{7,5,4,3,2,1,6,0:T(8,128)(2,1)S(1)}, u32[]{:S(2)}, u32[]{:S(2)}) %collective-permute-start.7) | collective-permute-done | bytes 393248 | tf_op jit(solution)/shard_map/ppermute | solution.py:13
  280.8 1.9 multiply_convert_fusion.1
  283.5 1.1 copy.25
  284.7 34.9 %reduce-scatter.2.cloned.1.call-done = bf16[192,512]{1,0:T(8,128)(2,1)} async-done(((bf16[192,2048]{1,0:T(8,128)(2,1)}), bf16[192,512]{1,0:T(8,128)(2,1)}) %reduce-scatter.2.cloned.1.call-update) | async-done | bytes 196624 | tf_op jit(solution)/shard_map/reduce_scatter | solution.py:134
  319.6 3.2 fusion.23
  322.9 3.1 convolution_add_fusion
  326.0 1.4 add_convert_fusion
  327.4 59.1 %all-reduce.2.cloned.1.call-done = bf16[4,48,3072]{2,1,0:T(8,128)(2,1)} async-done(((bf16[4,48,3072]{2,1,0:T(8,128)(2,1)}), bf16[4,48,3072]{2,1,0:T(8,128)(2,1)}) %all-reduce.2.cloned.1.call-update) | async-done | bytes 1179664 | tf_op jit(solution)/shard_map/psum | solution.py:152
  386.5 1.8 multiply_reduce_fusion.1
  390.5 2.8 fusion.15
  393.3 8.7 %all_gather.3 = bf16[192,2048]{1,0:T(8,128)(2,1)S(1)} all-gather(bf16[192,512]{1,0:T(8,128)(2,1)S(1)} %fusion.15), channel_id=1, replica_groups=mesh['seq'=128,'branch'=4] {'branch'}, dimensions={1}, use_global_device_ids=true | all-gather | bytes 983040 | tf_op jit(solution)/shard_map/all_gather | solution.py:162
  402.0 1.6 fusion.20
  403.8 0.8 multiply_convert_fusion.2
  (63 shorter events, 9.5 us)
Async XLA Ops:
  7.9 1.7 copy-start.5
  12.4 1.3 copy-start.4
  17.7 28.0 %collective-permute-start = (bf16[3,2,2,2,1,192,1,128]{7,5,4,3,2,1,6,0:T(8,128)(2,1)}, bf16[3,2,2,2,1,192,1,128]{7,5,4,3,2,1,6,0:T(8,128)(2,1)S(1)}, u32[]{:S(2)}, u32[]{:S(2)}) collective-permute-start(bf16[3,2,2,2,1,192,1,128]{7,5,4,3,2,1,6,0:T(8,128)(2,1)} %constant_dynamic-slice_fusion.7), channel_id=1, source_target_pairs={{0,4},{4,0},{8,12},{12,8},{16,20},{20,16},{24,28},{28,24},{32,36},... | collective-permute-start | bytes 3538952 | tf_op jit(solution)/shard_map/ppermute | solution.py:13
  47.1 31.3 %collective-permute-start.1 = (bf16[3,2,2,1,2,192,1,128]{7,5,4,3,2,1,6,0:T(8,128)(2,1)}, bf16[3,2,2,1,2,192,1,128]{7,5,4,3,2,1,6,0:T(8,128)(2,1)S(1)}, u32[]{:S(2)}, u32[]{:S(2)}) collective-permute-start(bf16[3,2,2,1,2,192,1,128]{7,5,4,3,2,1,6,0:T(8,128)(2,1)} %constant_dynamic-slice_fusion.6), channel_id=1, source_target_pairs={{0,8},{4,12},{8,0},{12,4},{16,24},{20,28},{24,16},{28,20},{32,40},... | collective-permute-start | bytes 3538952 | tf_op jit(solution)/shard_map/ppermute | solution.py:13
  79.7 28.9 %collective-permute-start.2 = (bf16[3,2,1,2,2,192,1,128]{7,5,4,3,2,1,6,0:T(8,128)(2,1)}, bf16[3,2,1,2,2,192,1,128]{7,5,4,3,2,1,6,0:T(8,128)(2,1)S(1)}, u32[]{:S(2)}, u32[]{:S(2)}) collective-permute-start(bf16[3,2,1,2,2,192,1,128]{7,5,4,3,2,1,6,0:T(8,128)(2,1)} %constant_dynamic-slice_fusion.5), channel_id=1, source_target_pairs={{0,16},{4,20},{8,24},{12,28},{16,0},{20,4},{24,8},{28,12},{32,48},... | collective-permute-start | bytes 3538952 | tf_op jit(solution)/shard_map/ppermute | solution.py:13
  84.6 28.8 %copy-start.8 = (bf16[512,24]{0,1:T(8,128)(2,1)S(1)}, bf16[512,24]{0,1:T(8,128)(2,1)}, u32[]{:S(2)}) copy-start(bf16[512,24]{0,1:T(8,128)(2,1)} %param.18) | copy-start | bytes 73732
  109.9 27.3 %collective-permute-start.3 = (bf16[3,1,2,2,2,192,1,128]{7,5,4,3,2,1,6,0:T(8,128)(2,1)}, bf16[3,1,2,2,2,192,1,128]{7,5,4,3,2,1,6,0:T(8,128)(2,1)S(1)}, u32[]{:S(2)}, u32[]{:S(2)}) collective-permute-start(bf16[3,1,2,2,2,192,1,128]{7,5,4,3,2,1,6,0:T(8,128)(2,1)} %constant_dynamic-slice_fusion.4), channel_id=1, source_target_pairs={{0,32},{4,36},{8,40},{12,44},{16,48},{20,52},{24,56},{28,60},{32,0... | collective-permute-start | bytes 3538952 | tf_op jit(solution)/shard_map/ppermute | solution.py:13
  115.3 204.4 %all-to-all-start = ((bf16[128,512,24]{1,2,0:T(8,128)(2,1)}), bf16[128,512,24]{1,2,0:T(8,128)(2,1)}, u32[]{:S(2)}, u32[]{:S(2)}) async-start(bf16[128,512,24]{1,2,0:T(8,128)(2,1)} %stack.14), calls=%async_computation.1 | async-start | bytes 6291456 | tf_op jit(solution)/shard_map/all_to_all | solution.py:133
  136.9 182.7 %reduce-scatter.2.cloned.1.call-start = ((), (), s32[]{:S(2)}) async-start(), calls=%async_computation.2 | async-start | bytes 983040 | tf_op jit(solution)/shard_map/reduce_scatter | solution.py:134
  140.7 1.2 copy-start.2
  145.9 1.2 copy-start.2
  151.1 1.2 copy-start.2
  156.3 1.2 copy-start.2
  161.5 1.2 copy-start.2
  166.7 1.2 copy-start.2
  171.0 42.7 %copy-start.9 = (f32[64]{0:T(128)S(1)}, f32[64]{0:T(128)}, u32[]{:S(2)}) copy-start(f32[64]{0:T(128)} %param.17) | copy-start | bytes 772
  171.0 11.8 %collective-permute-start.4 = (bf16[1,2,2,2,1,192,1,128]{7,5,4,3,2,1,6,0:T(8,128)(2,1)S(1)}, bf16[1,2,2,2,1,192,1,128]{7,5,4,3,2,1,6,0:T(8,128)(2,1)S(1)}, u32[]{:S(2)}, u32[]{:S(2)}) collective-permute-start(bf16[1,2,2,2,1,192,1,128]{7,5,4,3,2,1,6,0:T(8,128)(2,1)S(1)} %constant_dynamic-slice_fusion.3), channel_id=1, source_target_pairs={{0,4},{4,0},{8,12},{12,8},{16,20},{20,16},{24,28},{28,24},{32,36},... | collective-permute-start | bytes 1179656 | tf_op jit(solution)/shard_map/ppermute | solution.py:13
  184.6 10.4 %collective-permute-start.5 = (bf16[1,2,2,1,2,192,1,128]{7,5,4,3,2,1,6,0:T(8,128)(2,1)S(1)}, bf16[1,2,2,1,2,192,1,128]{7,5,4,3,2,1,6,0:T(8,128)(2,1)S(1)}, u32[]{:S(2)}, u32[]{:S(2)}) collective-permute-start(bf16[1,2,2,1,2,192,1,128]{7,5,4,3,2,1,6,0:T(8,128)(2,1)S(1)} %constant_dynamic-slice_fusion.2), channel_id=1, source_target_pairs={{0,8},{4,12},{8,0},{12,4},{16,24},{20,28},{24,16},{28,20},{32,40},... | collective-permute-start | bytes 1179656 | tf_op jit(solution)/shard_map/ppermute | solution.py:13
  196.9 12.3 %collective-permute-start.6 = (bf16[1,2,1,2,2,192,1,128]{7,5,4,3,2,1,6,0:T(8,128)(2,1)S(1)}, bf16[1,2,1,2,2,192,1,128]{7,5,4,3,2,1,6,0:T(8,128)(2,1)S(1)}, u32[]{:S(2)}, u32[]{:S(2)}) collective-permute-start(bf16[1,2,1,2,2,192,1,128]{7,5,4,3,2,1,6,0:T(8,128)(2,1)S(1)} %constant_dynamic-slice_fusion.1), channel_id=1, source_target_pairs={{0,16},{4,20},{8,24},{12,28},{16,0},{20,4},{24,8},{28,12},{32,48},... | collective-permute-start | bytes 1179656 | tf_op jit(solution)/shard_map/ppermute | solution.py:13
  211.1 68.9 %collective-permute-start.7 = (bf16[1,1,2,2,2,192,1,128]{7,5,4,3,2,1,6,0:T(8,128)(2,1)S(1)}, bf16[1,1,2,2,2,192,1,128]{7,5,4,3,2,1,6,0:T(8,128)(2,1)S(1)}, u32[]{:S(2)}, u32[]{:S(2)}) collective-permute-start(bf16[1,1,2,2,2,192,1,128]{7,5,4,3,2,1,6,0:T(8,128)(2,1)S(1)} %constant_dynamic-slice_fusion), channel_id=1, source_target_pairs={{0,32},{4,36},{8,40},{12,44},{16,48},{20,52},{24,56},{28,60},{32,0... | collective-permute-start | bytes 1179656 | tf_op jit(solution)/shard_map/ppermute | solution.py:13
  282.7 2.0 copy-start.6
  284.6 101.8 %all-reduce.2.cloned.1.call-start = ((), (), s32[]{:S(2)}) async-start(), calls=%async_computation.3 | async-start | bytes 2359296 | tf_op jit(solution)/shard_map/psum | solution.py:152
  319.6 3.2 copy-start.3
  326.0 60.5 %copy-start.1 = (bf16[192,3072]{1,0:T(8,128)(2,1)S(1)}, bf16[192,3072]{1,0:T(8,128)(2,1)}, u32[]{:S(2)}) copy-start(bf16[192,3072]{1,0:T(8,128)(2,1)} %param.21) | copy-start | bytes 3538948
  326.0 60.5 %copy-start.7 = (f32[3072]{0:T(1024)S(1)}, f32[3072]{0:T(1024)}, u32[]{:S(2)}) copy-start(f32[3072]{0:T(1024)} %param.20) | copy-start | bytes 36868
  386.5 2.4 copy-start
Sparse Core Ops, SparseCore 0:
  284.7 34.8 reduce-scatter.1
  327.5 58.8 all-reduce.1
